TPU v7x, 512 devices: a whole 4x4x16 slice. The times are simulated.
512 devices in a mesh: chain: 32 (over y, z_lo, core), block: 16 (over z_hi, x).
Axes of the slice: x: 4, y: 4, z: 16 (z_hi: 4, z_lo: 4; z = z_hi * 4 + z_lo), core: 2. Of those that a mesh axis runs over, the one named last changes fastest.
Arguments:
- state: bfloat16 [32, 16, 512, 512], P('chain', 'block'), may hold values from -400 to 400
- left_env: bfloat16 [32, 16, 2, 512, 512], P('chain', 'block'), may hold values from -1 to 5
- right_env: bfloat16 [32, 16, 2, 512, 512], P('chain', 'block'), may hold values from -1 to 5
- precond: float32 [32, 16, 512, 512], P('chain', 'block'), may hold values from 0.2 to 1
- ranks: int32 [32], P('chain'), may hold values from 1024 to 2048
Outputs:
- bond_out: bfloat16 [32, 16, 512, 512], P('chain', 'block')
All inputs are finite; a program needn't handle non-finite values.
Results may differ from a plain program's by a relative error of at most 0.0063.
Values may be sent and summed in bfloat16 or wider, within the bound.
No kernel may reach another device: no remote copies, remote signals or barrier semaphores. Data moves between devices by JAX's collectives and lax.ppermute only.
A program may use at most 64 MiB of HBM per device.

v0:
```python
import math
import jax
import jax.numpy as jnp
from jax import lax
from jax.sharding import Mesh
from jax.sharding import PartitionSpec as P

BLOCK = ("block_0", "block_1")


def from_partner(value, axis, distance):
    mask = 2**distance
    pairs = [(source, source ^ mask) for source in range(lax.axis_size(axis))]
    return lax.ppermute(value, axis, pairs)


def one_axis_at_a_time(x, axes):
    for axis in axes:
        x = lax.psum(x, axis)
    return x


def from_behind(value, axis, steps):
    count = lax.axis_size(axis)
    pairs = [(source, (source + steps) % count) for source in range(count)]
    return lax.ppermute(value, axis, pairs)


def join_halves(gathered, partner, position, bit_number, along):
    lower_half = position >> bit_number & 1 == 0
    first_way = jnp.concatenate([gathered, partner], along)
    second_way = jnp.concatenate([partner, gathered], along)
    return jnp.where(lower_half, first_way, second_way)


def unreverse(gathered, along, levels):
    shape = gathered.shape
    split_shape = shape[:along] + (2,) * levels + (shape[along] // 2**levels,) + shape[along + 1 :]
    order = (
        list(range(along))
        + list(range(along + levels - 1, along - 1, -1))
        + list(range(along + levels, len(split_shape)))
    )
    return gathered.reshape(split_shape).transpose(order).reshape(shape)


def gather_state_rows(gathered, position, levels):
    for level in range(levels):
        partner = from_partner(gathered, BLOCK, level)
        gathered = join_halves(gathered, partner, position, level, 1)
    return gathered


def gather_left_rows(gathered, position, levels):
    for level in range(levels):
        partner = from_partner(gathered, BLOCK, level)
        gathered = join_halves(gathered, partner, position, level, 2)
    return gathered


def gather_right_cols(gathered, position, levels):
    for level in range(levels):
        partner = from_partner(gathered, BLOCK, levels + level)
        gathered = join_halves(gathered, partner, position, levels + level, 1)
    return gathered


def gather_mid_cols(gathered, position, levels):
    level_order = list(range(levels - 1, -1, -1))
    for level in level_order:
        partner = from_partner(gathered, BLOCK, levels + level)
        gathered = join_halves(gathered, partner, position, levels + level, 1)
    gathered = unreverse(gathered, 1, levels)
    return gathered


def mix_weighted(first_tile, second_tile, first_weight, second_weight):
    return (
        first_weight * first_tile.astype(jnp.float32)
        + second_weight * second_tile.astype(jnp.float32)
    ).astype(jnp.bfloat16)


def per_device(state, left_env, right_env, precond, ranks):
    grid_side = math.isqrt(lax.axis_size(BLOCK))
    levels = grid_side.bit_length() - 1
    position = lax.axis_index(BLOCK)
    state_tile = state[0, 0]
    left_tiles = left_env[0, 0]
    right_tiles = right_env[0, 0]
    scaling = precond[0, 0]
    width = state_tile.shape[0]
    order_full = grid_side * width
    state_rows = gather_state_rows(state_tile, position, levels)
    left_rows = gather_left_rows(left_tiles, position, levels)
    right_cols = gather_right_cols(right_tiles, position, levels)
    middle = jnp.einsum(
        "ij,kjl->kil", state_rows, right_cols, preferred_element_type=jnp.float32
    ).astype(jnp.bfloat16)
    middle_cols = gather_mid_cols(middle, position, levels)
    image = jnp.einsum("kij,kjl->il", left_rows, middle_cols, preferred_element_type=jnp.float32)
    state_f = state_tile.astype(jnp.float32)
    row_index = position // grid_side * width + jnp.arange(width, dtype=jnp.int32)
    col_index = position % grid_side * width + jnp.arange(width, dtype=jnp.int32)
    rank_limit = ranks[0]
    keep_mask = ((row_index[:, None] < rank_limit) & (col_index[None, :] < rank_limit)).astype(
        jnp.float32
    )
    total_count = float(order_full * order_full)
    weighted = keep_mask * scaling
    state_sq = state_f * state_f
    cross_term = state_f * image
    moment_terms = (
        jnp.sum(state_sq),
        jnp.sum(cross_term),
        jnp.sum(keep_mask * state_sq),
        jnp.sum(weighted * state_sq),
        jnp.sum(weighted * scaling * state_sq),
        jnp.sum(weighted * cross_term),
        jnp.sum(weighted * scaling * cross_term),
        jnp.sum(weighted * scaling * image * image),
    )
    norm_state, intersection, plain_sq, first_sq, second_sq, first_cross, second_cross, image_sq = (
        one_axis_at_a_time(moment_terms[0], BLOCK),
        one_axis_at_a_time(moment_terms[1], BLOCK),
        one_axis_at_a_time(moment_terms[2], BLOCK),
        one_axis_at_a_time(moment_terms[3], BLOCK),
        one_axis_at_a_time(moment_terms[4], BLOCK),
        one_axis_at_a_time(moment_terms[5], BLOCK),
        one_axis_at_a_time(moment_terms[6], BLOCK),
        one_axis_at_a_time(moment_terms[7], BLOCK),
    )
    energy = intersection / norm_state
    corrected = keep_mask * (state_f - (image - energy * state_f) * scaling)
    square_sum = (
        plain_sq
        + 2.0 * energy * first_sq
        + energy * energy * second_sq
        - 2.0 * first_cross
        - 2.0 * energy * second_cross
        + image_sq
    )
    bond = (corrected / jnp.sqrt(square_sum / total_count + 1e-06)).astype(jnp.bfloat16)
    partner = from_partner(bond, "chain", 0)
    own_pair = mix_weighted(bond, partner, 0.75, 0.25)
    ahead = from_behind(own_pair, "chain", -1)
    crossed = from_partner(ahead, "chain", 0)
    other_pair = from_behind(crossed, "chain", 1)
    result = mix_weighted(own_pair, other_pair, 0.5, 0.5)
    return result[None, None]


def solution(mesh):
    split = Mesh(mesh.devices.reshape(mesh.shape["chain"], 4, 4), ("chain", "block_0", "block_1"))
    placed = (
        P("chain", BLOCK, None, None),
        P("chain", BLOCK, None, None, None),
        P("chain", BLOCK, None, None, None),
        P("chain", BLOCK, None, None),
        P("chain"),
    )
    return jax.shard_map(
        per_device,
        mesh=split,
        in_specs=placed,
        out_specs=P("chain", BLOCK, None, None),
        check_vma=False,
    )
```

profile of v0, /device:TPU:2, one launch (start us, length us, event | category | flops | bytes accessed | tf_op | source)
XLA Modules:
  0.0 672.2 jit_solution(9116957013693709141)
XLA Ops:
  0.0 9.2 %collective-permute-start.2 = (bf16[2,512,512]{2,1,0:T(8,128)(2,1)}, bf16[2,512,512]{2,1,0:T(8,128)(2,1)}, u32[]{:S(2)}, u32[]{:S(2)}) collective-permute-start(bf16[2,512,512]{2,1,0:T(8,128)(2,1)} %bitcast.46), channel_id=1, source_target_pairs={{0,4},{1,5},{2,6},{3,7},{4,0},{5,1},{6,2},{7,3},{8,12},{9,13},{10,... | collective-permute-start | bytes 3145736 | tf_op jit(solution)/shard_map/ppermute | solution.py:14
  9.2 136.1 %collective-permute-done.2 = bf16[2,512,512]{2,1,0:T(8,128)(2,1)} collective-permute-done((bf16[2,512,512]{2,1,0:T(8,128)(2,1)}, bf16[2,512,512]{2,1,0:T(8,128)(2,1)}, u32[]{:S(2)}, u32[]{:S(2)}) %collective-permute-start.2) | collective-permute-done | bytes 1048608 | tf_op jit(solution)/shard_map/ppermute | solution.py:14
  145.3 2.8 maximum_select_fusion.7
  148.2 127.8 %collective-permute-start.3 = (bf16[2,1024,512]{2,1,0:T(8,128)(2,1)S(1)}, bf16[2,1024,512]{2,1,0:T(8,128)(2,1)}, u32[]{:S(2)}, u32[]{:S(2)}) collective-permute-start(bf16[2,1024,512]{2,1,0:T(8,128)(2,1)S(1)} %maximum_select_fusion.7), channel_id=1, source_target_pairs={{0,8},{1,9},{2,10},{3,11},{4,12},{5,13},{6,14},{7,15},{8,0},{9,1},... | collective-permute-start | bytes 6291464 | tf_op jit(solution)/shard_map/ppermute | solution.py:14
  276.0 2.4 collective-permute-start.4
  278.5 12.5 %collective-permute-done.4 = bf16[512,512]{1,0:T(8,128)(2,1)S(1)} collective-permute-done((bf16[512,512]{1,0:T(8,128)(2,1)S(1)}, bf16[512,512]{1,0:T(8,128)(2,1)S(1)}, u32[]{:S(2)}, u32[]{:S(2)}) %collective-permute-start.4) | collective-permute-done | bytes 524320 | tf_op jit(solution)/shard_map/ppermute | solution.py:14
  292.3 4.0 collective-permute-start.5
  296.3 23.2 %collective-permute-done.5 = bf16[512,1024]{1,0:T(8,128)(2,1)} collective-permute-done((bf16[512,1024]{1,0:T(8,128)(2,1)}, bf16[512,1024]{1,0:T(8,128)(2,1)}, u32[]{:S(2)}, u32[]{:S(2)}) %collective-permute-start.5) | collective-permute-done | bytes 1048608 | tf_op jit(solution)/shard_map/ppermute | solution.py:14
  319.6 2.2 collective-permute-done.3
  321.8 5.9 fusion.29
  327.6 12.2 %collective-permute-start.6 = (bf16[2,512,512]{2,1,0:T(8,128)(2,1)S(1)}, bf16[2,512,512]{2,1,0:T(8,128)(2,1)S(1)}, u32[]{:S(2)}, u32[]{:S(2)}) collective-permute-start(bf16[2,512,512]{2,1,0:T(8,128)(2,1)S(1)} %fusion.29), channel_id=1, source_target_pairs={{0,8},{1,9},{2,10},{3,11},{4,12},{5,13},{6,14},{7,15},{8,0},{9,1},... | collective-permute-start | bytes 3145736 | tf_op jit(solution)/shard_map/ppermute | solution.py:14
  339.9 2.4 collective-permute-start
  342.4 19.9 %collective-permute-done.6 = bf16[2,512,512]{2,1,0:T(8,128)(2,1)S(1)} collective-permute-done((bf16[2,512,512]{2,1,0:T(8,128)(2,1)S(1)}, bf16[2,512,512]{2,1,0:T(8,128)(2,1)S(1)}, u32[]{:S(2)}, u32[]{:S(2)}) %collective-permute-start.6) | collective-permute-done | bytes 1048608 | tf_op jit(solution)/shard_map/ppermute | solution.py:14
  362.9 170.4 %collective-permute-start.7 = (bf16[2,1024,512]{2,1,0:T(8,128)(2,1)S(1)}, bf16[2,1024,512]{2,1,0:T(8,128)(2,1)}, u32[]{:S(2)}, u32[]{:S(2)}) collective-permute-start(bf16[2,1024,512]{2,1,0:T(8,128)(2,1)S(1)} %maximum_select_fusion.8), channel_id=1, source_target_pairs={{0,4},{1,5},{2,6},{3,7},{4,0},{5,1},{6,2},{7,3},{8,12},{9,13},{10,... | collective-permute-start | bytes 6291464 | tf_op jit(solution)/shard_map/ppermute | solution.py:14
  535.4 4.0 collective-permute-start.1
  540.1 39.1 %collective-permute-done.7 = bf16[2,1024,512]{2,1,0:T(8,128)(2,1)} collective-permute-done((bf16[2,1024,512]{2,1,0:T(8,128)(2,1)S(1)}, bf16[2,1024,512]{2,1,0:T(8,128)(2,1)}, u32[]{:S(2)}, u32[]{:S(2)}) %collective-permute-start.7) | collective-permute-done | bytes 2097184 | tf_op jit(solution)/shard_map/ppermute | solution.py:14
  579.2 3.3 maximum_select_fusion.4
  582.8 3.5 collective-permute-done.1
  586.3 5.9 multiply_reduce_fusion
  592.1 14.3 %all-reduce.1 = (f32[]{:T(128)}, f32[]{:T(128)}, f32[]{:T(128)}, f32[]{:T(128)}, f32[]{:T(128)}, /*index=5*/f32[]{:T(128)}, f32[]{:T(128)}, f32[]{:T(128)}) all-reduce(f32[]{:T(128)} %get-tuple-element.11, f32[]{:T(128)} %get-tuple-element.10, f32[]{:T(128)} %get-tuple-element.12, ...), channel_id=1, replica_groups=mesh['chain'=32,'block_0'=4,'block_1'=4] {'block_0'}, use_global_device_ids=true, to_apply=%region_7.8 | all-reduce | flops 8 | bytes 64 | tf_op jit(solution)/shard_map/psum | solution.py:19
  606.5 9.3 %all-reduce = (f32[]{:T(128)}, f32[]{:T(128)}, f32[]{:T(128)}, f32[]{:T(128)}, f32[]{:T(128)}, /*index=5*/f32[]{:T(128)}, f32[]{:T(128)}, f32[]{:T(128)}) all-reduce(f32[]{:T(128)} %get-tuple-element.21, f32[]{:T(128)} %get-tuple-element.22, f32[]{:T(128)} %get-tuple-element.23, ...), channel_id=1, replica_groups=mesh['chain'=32,'block_0'=4,'block_1'=4] {'block_1'}, use_global_device_ids=true, to_apply=%region_8.9 | all-reduce | flops 8 | bytes 64 | tf_op jit(solution)/shard_map/psum | solution.py:19
  625.3 20.9 %collective-permute-start.9 = (bf16[512,512]{1,0:T(8,128)(2,1)S(1)}, bf16[512,512]{1,0:T(8,128)(2,1)S(1)}, u32[]{:S(2)}, u32[]{:S(2)}) collective-permute-start(bf16[512,512]{1,0:T(8,128)(2,1)S(1)} %add_convert_fusion), channel_id=1, source_target_pairs={{0,496},{16,0},{32,16},{48,32},{64,48},{80,64},{96,80},{112,96},{1... | collective-permute-start | bytes 1572872 | tf_op jit(solution)/shard_map/ppermute | solution.py:26
  646.2 6.7 collective-permute-done.9
  658.7 12.5 %collective-permute-done.11 = bf16[512,512]{1,0:T(8,128)(2,1)S(1)} collective-permute-done((bf16[512,512]{1,0:T(8,128)(2,1)S(1)}, bf16[512,512]{1,0:T(8,128)(2,1)S(1)}, u32[]{:S(2)}, u32[]{:S(2)}) %collective-permute-start.11) | collective-permute-done | bytes 524320 | tf_op jit(solution)/shard_map/ppermute | solution.py:26
  (20 shorter events, 15.4 us)
Async XLA Ops:
  0.0 276.0 %copy-start = (bf16[1,1,512,512]{3,2,1,0:T(8,128)(2,1)S(1)}, bf16[1,1,512,512]{3,2,1,0:T(8,128)(2,1)}, u32[]{:S(2)}) copy-start(bf16[1,1,512,512]{3,2,1,0:T(8,128)(2,1)} %param.5) | copy-start | bytes 1572868
  0.0 145.3 %collective-permute-start.2 = (bf16[2,512,512]{2,1,0:T(8,128)(2,1)}, bf16[2,512,512]{2,1,0:T(8,128)(2,1)}, u32[]{:S(2)}, u32[]{:S(2)}) collective-permute-start(bf16[2,512,512]{2,1,0:T(8,128)(2,1)} %bitcast.46), channel_id=1, source_target_pairs={{0,4},{1,5},{2,6},{3,7},{4,0},{5,1},{6,2},{7,3},{8,12},{9,13},{10,... | collective-permute-start | bytes 3145736 | tf_op jit(solution)/shard_map/ppermute | solution.py:14
  148.2 173.6 %collective-permute-start.3 = (bf16[2,1024,512]{2,1,0:T(8,128)(2,1)S(1)}, bf16[2,1024,512]{2,1,0:T(8,128)(2,1)}, u32[]{:S(2)}, u32[]{:S(2)}) collective-permute-start(bf16[2,1024,512]{2,1,0:T(8,128)(2,1)S(1)} %maximum_select_fusion.7), channel_id=1, source_target_pairs={{0,8},{1,9},{2,10},{3,11},{4,12},{5,13},{6,14},{7,15},{8,0},{9,1},... | collective-permute-start | bytes 6291464 | tf_op jit(solution)/shard_map/ppermute | solution.py:14
  276.0 15.0 %collective-permute-start.4 = (bf16[512,512]{1,0:T(8,128)(2,1)S(1)}, bf16[512,512]{1,0:T(8,128)(2,1)S(1)}, u32[]{:S(2)}, u32[]{:S(2)}) collective-permute-start(bf16[512,512]{1,0:T(8,128)(2,1)S(1)} %bitcast.44), channel_id=1, source_target_pairs={{0,1},{1,0},{2,3},{3,2},{4,5},{5,4},{6,7},{7,6},{8,9},{9,8},{10,11... | collective-permute-start | bytes 1572872 | tf_op jit(solution)/shard_map/ppermute | solution.py:14
  292.3 27.3 %collective-permute-start.5 = (bf16[512,1024]{1,0:T(8,128)(2,1)}, bf16[512,1024]{1,0:T(8,128)(2,1)}, u32[]{:S(2)}, u32[]{:S(2)}) collective-permute-start(bf16[512,1024]{1,0:T(8,128)(2,1)} %maximum_select_fusion.15), channel_id=1, source_target_pairs={{0,2},{1,3},{2,0},{3,1},{4,6},{5,7},{6,4},{7,5},{8,10},{9,11},{10,... | collective-permute-start | bytes 3145736 | tf_op jit(solution)/shard_map/ppermute | solution.py:14
  296.3 43.6 %copy-start.1 = (bf16[1,1,2,512,512]{4,3,2,1,0:T(8,128)(2,1)S(1)}, bf16[1,1,2,512,512]{4,3,2,1,0:T(8,128)(2,1)}, u32[]{:S(2)}) copy-start(bf16[1,1,2,512,512]{4,3,2,1,0:T(8,128)(2,1)} %param.6) | copy-start | bytes 3145732
  327.6 34.6 %collective-permute-start.6 = (bf16[2,512,512]{2,1,0:T(8,128)(2,1)S(1)}, bf16[2,512,512]{2,1,0:T(8,128)(2,1)S(1)}, u32[]{:S(2)}, u32[]{:S(2)}) collective-permute-start(bf16[2,512,512]{2,1,0:T(8,128)(2,1)S(1)} %fusion.29), channel_id=1, source_target_pairs={{0,8},{1,9},{2,10},{3,11},{4,12},{5,13},{6,14},{7,15},{8,0},{9,1},... | collective-permute-start | bytes 3145736 | tf_op jit(solution)/shard_map/ppermute | solution.py:14
  339.9 193.5 %collective-permute-start = (bf16[2,512,512]{2,1,0:T(8,128)(2,1)S(1)}, bf16[2,512,512]{2,1,0:T(8,128)(2,1)S(1)}, u32[]{:S(2)}, u32[]{:S(2)}) collective-permute-start(bf16[2,512,512]{2,1,0:T(8,128)(2,1)S(1)} %bitcast.48), channel_id=1, source_target_pairs={{0,1},{1,0},{2,3},{3,2},{4,5},{5,4},{6,7},{7,6},{8,9},{9,8},{10,11... | collective-permute-start | bytes 3145736 | tf_op jit(solution)/shard_map/ppermute | solution.py:14
  362.9 216.2 %collective-permute-start.7 = (bf16[2,1024,512]{2,1,0:T(8,128)(2,1)S(1)}, bf16[2,1024,512]{2,1,0:T(8,128)(2,1)}, u32[]{:S(2)}, u32[]{:S(2)}) collective-permute-start(bf16[2,1024,512]{2,1,0:T(8,128)(2,1)S(1)} %maximum_select_fusion.8), channel_id=1, source_target_pairs={{0,4},{1,5},{2,6},{3,7},{4,0},{5,1},{6,2},{7,3},{8,12},{9,13},{10,... | collective-permute-start | bytes 6291464 | tf_op jit(solution)/shard_map/ppermute | solution.py:14
  535.4 50.9 %collective-permute-start.1 = (bf16[2,512,1024]{2,1,0:T(8,128)(2,1)}, bf16[2,512,1024]{2,1,0:T(8,128)(2,1)}, u32[]{:S(2)}, u32[]{:S(2)}) collective-permute-start(bf16[2,512,1024]{2,1,0:T(8,128)(2,1)} %maximum_select_fusion.5), channel_id=1, source_target_pairs={{0,2},{1,3},{2,0},{3,1},{4,6},{5,7},{6,4},{7,5},{8,10},{9,11},{10,... | collective-permute-start | bytes 6291464 | tf_op jit(solution)/shard_map/ppermute | solution.py:14
  582.5 3.8 copy-start.2
  621.3 3.8 collective-permute-start.8
  625.3 27.6 %collective-permute-start.9 = (bf16[512,512]{1,0:T(8,128)(2,1)S(1)}, bf16[512,512]{1,0:T(8,128)(2,1)S(1)}, u32[]{:S(2)}, u32[]{:S(2)}) collective-permute-start(bf16[512,512]{1,0:T(8,128)(2,1)S(1)} %add_convert_fusion), channel_id=1, source_target_pairs={{0,496},{16,0},{32,16},{48,32},{64,48},{80,64},{96,80},{112,96},{1... | collective-permute-start | bytes 1572872 | tf_op jit(solution)/shard_map/ppermute | solution.py:26
  652.9 3.8 collective-permute-start.10
  656.7 14.6 %collective-permute-start.11 = (bf16[512,512]{1,0:T(8,128)(2,1)S(1)}, bf16[512,512]{1,0:T(8,128)(2,1)S(1)}, u32[]{:S(2)}, u32[]{:S(2)}) collective-permute-start(bf16[512,512]{1,0:T(8,128)(2,1)S(1)} %collective-permute-done.10), channel_id=1, source_target_pairs={{0,16},{16,32},{32,48},{48,64},{64,80},{80,96},{96,112},{112,128},... | collective-permute-start | bytes 1572872 | tf_op jit(solution)/shard_map/ppermute | solution.py:26
where the time goes:
time: 673 us; the launch traced here: 672 us
  starting transfers between devices  359 us (53%)
  waiting for transfers between devices  259 us (38%)
  blocking collectives  23.6 us (4%)
  matrix products  11.7 us (2%)
  other arithmetic  11.6 us (2%)
    ppermute x10, starting transfers between devices, from_partner(): return lax.ppermute(value, axis, pairs)  336 us
    ppermute x10, waiting for transfers between devices, from_partner(): return lax.ppermute(value, axis, pairs)  240 us
    psum x2, blocking collectives, one_axis_at_a_time(): x = lax.psum(x, axis)  23.6 us
    ppermute x2, starting transfers between devices, from_behind(): return lax.ppermute(value, axis, pairs)  23 us
    ppermute x2, waiting for transfers between devices, from_behind(): return lax.ppermute(value, axis, pairs)  19.2 us
  transfers between devices with their start and end apart: 12, of which 11 were waited for; matrix products, arithmetic and copies ran while one was open for 1% of the time, Pallas kernels for 0%

commit v1 on v0

--- a/solution.py
+++ b/solution.py
@@ -16,7 +16,8 @@
 
 def one_axis_at_a_time(x, axes):
     for axis in axes:
-        x = lax.psum(x, axis)
+        blocks = lax.all_gather(x, axis, axis=0, tiled=False)
+        x = blocks.sum(axis=0)
     return x
 
 

time: 673 us -> 729 us (1.083)
  local copies, waits for them, and re-layouts: 0.29 us -> 48.5 us
  other arithmetic: 11.6 us -> 21.4 us
    unnamed x6 -> x40, local copies, waits for them, and re-layouts: 0.02 us -> 48.2 us
    psum x2 -> x0, blocking collectives: 23.6 us -> none  [one_axis_at_a_time(): x = lax.psum(x, axis)]
    unnamed x0 -> x2, blocking collectives: none -> 22.5 us
    reduce_sum x0 -> x16, other arithmetic: none -> 9.74 us  [one_axis_at_a_time(): x = blocks.sum(axis=0)]
where the time goes in v1:
time: 729 us; the launch traced here: 728 us
  starting transfers between devices  359 us (49%)
  waiting for transfers between devices  258 us (35%)
  local copies, waits for them, and re-layouts  48.5 us (7%)
  blocking collectives  22.5 us (3%)
  other arithmetic  21.4 us (3%)
  matrix products  11.8 us (2%)
    ppermute x10, starting transfers between devices, from_partner(): return lax.ppermute(value, axis, pairs)  337 us
    ppermute x10, waiting for transfers between devices, from_partner(): return lax.ppermute(value, axis, pairs)  239 us
    unnamed x40, local copies, waits for them, and re-layouts  48.2 us
    ppermute x2, starting transfers between devices, from_behind(): return lax.ppermute(value, axis, pairs)  22.9 us
    unnamed x2, blocking collectives  22.5 us
    ppermute x2, waiting for transfers between devices, from_behind(): return lax.ppermute(value, axis, pairs)  19.2 us
  transfers between devices with their start and end apart: 12, of which 11 were waited for; matrix products, arithmetic and copies ran while one was open for 1% of the time, Pallas kernels for 0%

profile of v1, /device:TPU:2, one launch (start us, length us, event | category | flops | bytes accessed | tf_op | source)
XLA Modules:
  0.0 728.1 jit_solution(13705474302662155650)
XLA Ops:
  0.0 9.2 %collective-permute-start.2 = (bf16[2,512,512]{2,1,0:T(8,128)(2,1)}, bf16[2,512,512]{2,1,0:T(8,128)(2,1)}, u32[]{:S(2)}, u32[]{:S(2)}) collective-permute-start(bf16[2,512,512]{2,1,0:T(8,128)(2,1)} %bitcast.64), channel_id=1, source_target_pairs={{0,4},{1,5},{2,6},{3,7},{4,0},{5,1},{6,2},{7,3},{8,12},{9,13},{10,... | collective-permute-start | bytes 3145736 | tf_op jit(solution)/shard_map/ppermute | solution.py:14
  9.2 136.1 %collective-permute-done.2 = bf16[2,512,512]{2,1,0:T(8,128)(2,1)} collective-permute-done((bf16[2,512,512]{2,1,0:T(8,128)(2,1)}, bf16[2,512,512]{2,1,0:T(8,128)(2,1)}, u32[]{:S(2)}, u32[]{:S(2)}) %collective-permute-start.2) | collective-permute-done | bytes 1048608 | tf_op jit(solution)/shard_map/ppermute | solution.py:14
  145.3 2.8 maximum_select_fusion.7
  148.2 127.8 %collective-permute-start.3 = (bf16[2,1024,512]{2,1,0:T(8,128)(2,1)S(1)}, bf16[2,1024,512]{2,1,0:T(8,128)(2,1)}, u32[]{:S(2)}, u32[]{:S(2)}) collective-permute-start(bf16[2,1024,512]{2,1,0:T(8,128)(2,1)S(1)} %maximum_select_fusion.7), channel_id=1, source_target_pairs={{0,8},{1,9},{2,10},{3,11},{4,12},{5,13},{6,14},{7,15},{8,0},{9,1},... | collective-permute-start | bytes 6291464 | tf_op jit(solution)/shard_map/ppermute | solution.py:14
  278.5 12.5 %collective-permute-done.4 = bf16[512,512]{1,0:T(8,128)(2,1)S(1)} collective-permute-done((bf16[512,512]{1,0:T(8,128)(2,1)S(1)}, bf16[512,512]{1,0:T(8,128)(2,1)S(1)}, u32[]{:S(2)}, u32[]{:S(2)}) %collective-permute-start.4) | collective-permute-done | bytes 524320 | tf_op jit(solution)/shard_map/ppermute | solution.py:14
  292.3 4.0 collective-permute-start.5
  296.3 23.2 %collective-permute-done.5 = bf16[512,1024]{1,0:T(8,128)(2,1)} collective-permute-done((bf16[512,1024]{1,0:T(8,128)(2,1)}, bf16[512,1024]{1,0:T(8,128)(2,1)}, u32[]{:S(2)}, u32[]{:S(2)}) %collective-permute-start.5) | collective-permute-done | bytes 1048608 | tf_op jit(solution)/shard_map/ppermute | solution.py:14
  321.8 5.9 fusion.29
  327.6 12.2 %collective-permute-start.6 = (bf16[2,512,512]{2,1,0:T(8,128)(2,1)S(1)}, bf16[2,512,512]{2,1,0:T(8,128)(2,1)S(1)}, u32[]{:S(2)}, u32[]{:S(2)}) collective-permute-start(bf16[2,512,512]{2,1,0:T(8,128)(2,1)S(1)} %fusion.29), channel_id=1, source_target_pairs={{0,8},{1,9},{2,10},{3,11},{4,12},{5,13},{6,14},{7,15},{8,0},{9,1},... | collective-permute-start | bytes 3145736 | tf_op jit(solution)/shard_map/ppermute | solution.py:14
  342.4 19.9 %collective-permute-done.6 = bf16[2,512,512]{2,1,0:T(8,128)(2,1)S(1)} collective-permute-done((bf16[2,512,512]{2,1,0:T(8,128)(2,1)S(1)}, bf16[2,512,512]{2,1,0:T(8,128)(2,1)S(1)}, u32[]{:S(2)}, u32[]{:S(2)}) %collective-permute-start.6) | collective-permute-done | bytes 1048608 | tf_op jit(solution)/shard_map/ppermute | solution.py:14
  362.9 170.5 %collective-permute-start.7 = (bf16[2,1024,512]{2,1,0:T(8,128)(2,1)S(1)}, bf16[2,1024,512]{2,1,0:T(8,128)(2,1)}, u32[]{:S(2)}, u32[]{:S(2)}) collective-permute-start(bf16[2,1024,512]{2,1,0:T(8,128)(2,1)S(1)} %maximum_select_fusion.8), channel_id=1, source_target_pairs={{0,4},{1,5},{2,6},{3,7},{4,0},{5,1},{6,2},{7,3},{8,12},{9,13},{10,... | collective-permute-start | bytes 6291464 | tf_op jit(solution)/shard_map/ppermute | solution.py:14
  535.4 4.0 collective-permute-start.1
  541.4 37.9 %collective-permute-done.7 = bf16[2,1024,512]{2,1,0:T(8,128)(2,1)} collective-permute-done((bf16[2,1024,512]{2,1,0:T(8,128)(2,1)S(1)}, bf16[2,1024,512]{2,1,0:T(8,128)(2,1)}, u32[]{:S(2)}, u32[]{:S(2)}) %collective-permute-start.7) | collective-permute-done | bytes 2097184 | tf_op jit(solution)/shard_map/ppermute | solution.py:14
  579.3 3.3 maximum_select_fusion.4
  582.9 3.5 collective-permute-done.1
  586.4 6.0 multiply_reduce_fusion
  616.0 13.8 %all-reduce.17 = (f32[4]{0:T(128)S(1)}, f32[4]{0:T(128)S(1)}, f32[4]{0:T(128)S(1)}, f32[4]{0:T(128)S(1)}, f32[4]{0:T(128)S(1)}, /*index=5*/f32[4]{0:T(128)S(1)}, f32[4]{0:T(128)S(1)}, f32[4]{0:T(128)S(1)}) all-reduce(f32[4]{0:T(128)} %dynamic-update-slice.4, ...), channel_id=1, replica_groups=mesh['chain'=32,'block_0'=4,'block_1'=4] {'block_0'}, use_global_device_ids=true, to_apply=%add.4 | all-reduce | flops 32 | bytes 256
  636.6 2.7 dynamic-update-slice.15
  640.5 2.6 dynamic-update-slice.3
  651.5 2.7 dynamic-update-slice.1
  657.9 8.7 %all-reduce.16 = (f32[4]{0:T(128)S(1)}, f32[4]{0:T(128)S(1)}, f32[4]{0:T(128)S(1)}, f32[4]{0:T(128)S(1)}, f32[4]{0:T(128)S(1)}, /*index=5*/f32[4]{0:T(128)S(1)}, f32[4]{0:T(128)S(1)}, f32[4]{0:T(128)S(1)}) all-reduce(f32[4]{0:T(128)} %dynamic-update-slice.5, ...), channel_id=1, replica_groups=mesh['chain'=32,'block_0'=4,'block_1'=4] {'block_1'}, use_global_device_ids=true, to_apply=%add.5 | all-reduce | flops 32 | bytes 256
  681.2 20.9 %collective-permute-start.9 = (bf16[512,512]{1,0:T(8,128)(2,1)S(1)}, bf16[512,512]{1,0:T(8,128)(2,1)S(1)}, u32[]{:S(2)}, u32[]{:S(2)}) collective-permute-start(bf16[512,512]{1,0:T(8,128)(2,1)S(1)} %add_convert_fusion), channel_id=1, source_target_pairs={{0,496},{16,0},{32,16},{48,32},{64,48},{80,64},{96,80},{112,96},{1... | collective-permute-start | bytes 1572872 | tf_op jit(solution)/shard_map/ppermute | solution.py:27
  702.1 6.7 collective-permute-done.9
  714.6 12.5 %collective-permute-done.11 = bf16[512,512]{1,0:T(8,128)(2,1)S(1)} collective-permute-done((bf16[512,512]{1,0:T(8,128)(2,1)S(1)}, bf16[512,512]{1,0:T(8,128)(2,1)S(1)}, u32[]{:S(2)}, u32[]{:S(2)}) %collective-permute-start.11) | collective-permute-done | bytes 524320 | tf_op jit(solution)/shard_map/ppermute | solution.py:27
  (70 shorter events, 72.5 us)
Async XLA Ops:
  0.0 276.0 %copy-start = (bf16[1,1,512,512]{3,2,1,0:T(8,128)(2,1)S(1)}, bf16[1,1,512,512]{3,2,1,0:T(8,128)(2,1)}, u32[]{:S(2)}) copy-start(bf16[1,1,512,512]{3,2,1,0:T(8,128)(2,1)} %param.5) | copy-start | bytes 1572868
  0.0 145.3 %collective-permute-start.2 = (bf16[2,512,512]{2,1,0:T(8,128)(2,1)}, bf16[2,512,512]{2,1,0:T(8,128)(2,1)}, u32[]{:S(2)}, u32[]{:S(2)}) collective-permute-start(bf16[2,512,512]{2,1,0:T(8,128)(2,1)} %bitcast.64), channel_id=1, source_target_pairs={{0,4},{1,5},{2,6},{3,7},{4,0},{5,1},{6,2},{7,3},{8,12},{9,13},{10,... | collective-permute-start | bytes 3145736 | tf_op jit(solution)/shard_map/ppermute | solution.py:14
  148.2 173.6 %collective-permute-start.3 = (bf16[2,1024,512]{2,1,0:T(8,128)(2,1)S(1)}, bf16[2,1024,512]{2,1,0:T(8,128)(2,1)}, u32[]{:S(2)}, u32[]{:S(2)}) collective-permute-start(bf16[2,1024,512]{2,1,0:T(8,128)(2,1)S(1)} %maximum_select_fusion.7), channel_id=1, source_target_pairs={{0,8},{1,9},{2,10},{3,11},{4,12},{5,13},{6,14},{7,15},{8,0},{9,1},... | collective-permute-start | bytes 6291464 | tf_op jit(solution)/shard_map/ppermute | solution.py:14
  276.0 15.0 %collective-permute-start.4 = (bf16[512,512]{1,0:T(8,128)(2,1)S(1)}, bf16[512,512]{1,0:T(8,128)(2,1)S(1)}, u32[]{:S(2)}, u32[]{:S(2)}) collective-permute-start(bf16[512,512]{1,0:T(8,128)(2,1)S(1)} %bitcast.62), channel_id=1, source_target_pairs={{0,1},{1,0},{2,3},{3,2},{4,5},{5,4},{6,7},{7,6},{8,9},{9,8},{10,11... | collective-permute-start | bytes 1572872 | tf_op jit(solution)/shard_map/ppermute | solution.py:14
  292.3 27.3 %collective-permute-start.5 = (bf16[512,1024]{1,0:T(8,128)(2,1)}, bf16[512,1024]{1,0:T(8,128)(2,1)}, u32[]{:S(2)}, u32[]{:S(2)}) collective-permute-start(bf16[512,1024]{1,0:T(8,128)(2,1)} %maximum_select_fusion.15), channel_id=1, source_target_pairs={{0,2},{1,3},{2,0},{3,1},{4,6},{5,7},{6,4},{7,5},{8,10},{9,11},{10,... | collective-permute-start | bytes 3145736 | tf_op jit(solution)/shard_map/ppermute | solution.py:14
  296.3 43.6 %copy-start.1 = (bf16[1,1,2,512,512]{4,3,2,1,0:T(8,128)(2,1)S(1)}, bf16[1,1,2,512,512]{4,3,2,1,0:T(8,128)(2,1)}, u32[]{:S(2)}) copy-start(bf16[1,1,2,512,512]{4,3,2,1,0:T(8,128)(2,1)} %param.6) | copy-start | bytes 3145732
  327.6 34.6 %collective-permute-start.6 = (bf16[2,512,512]{2,1,0:T(8,128)(2,1)S(1)}, bf16[2,512,512]{2,1,0:T(8,128)(2,1)S(1)}, u32[]{:S(2)}, u32[]{:S(2)}) collective-permute-start(bf16[2,512,512]{2,1,0:T(8,128)(2,1)S(1)} %fusion.29), channel_id=1, source_target_pairs={{0,8},{1,9},{2,10},{3,11},{4,12},{5,13},{6,14},{7,15},{8,0},{9,1},... | collective-permute-start | bytes 3145736 | tf_op jit(solution)/shard_map/ppermute | solution.py:14
  339.9 193.5 %collective-permute-start = (bf16[2,512,512]{2,1,0:T(8,128)(2,1)S(1)}, bf16[2,512,512]{2,1,0:T(8,128)(2,1)S(1)}, u32[]{:S(2)}, u32[]{:S(2)}) collective-permute-start(bf16[2,512,512]{2,1,0:T(8,128)(2,1)S(1)} %bitcast.66), channel_id=1, source_target_pairs={{0,1},{1,0},{2,3},{3,2},{4,5},{5,4},{6,7},{7,6},{8,9},{9,8},{10,11... | collective-permute-start | bytes 3145736 | tf_op jit(solution)/shard_map/ppermute | solution.py:14
  362.9 216.4 %collective-permute-start.7 = (bf16[2,1024,512]{2,1,0:T(8,128)(2,1)S(1)}, bf16[2,1024,512]{2,1,0:T(8,128)(2,1)}, u32[]{:S(2)}, u32[]{:S(2)}) collective-permute-start(bf16[2,1024,512]{2,1,0:T(8,128)(2,1)S(1)} %maximum_select_fusion.8), channel_id=1, source_target_pairs={{0,4},{1,5},{2,6},{3,7},{4,0},{5,1},{6,2},{7,3},{8,12},{9,13},{10,... | collective-permute-start | bytes 6291464 | tf_op jit(solution)/shard_map/ppermute | solution.py:14
  535.4 51.0 %collective-permute-start.1 = (bf16[2,512,1024]{2,1,0:T(8,128)(2,1)}, bf16[2,512,1024]{2,1,0:T(8,128)(2,1)}, u32[]{:S(2)}, u32[]{:S(2)}) collective-permute-start(bf16[2,512,1024]{2,1,0:T(8,128)(2,1)} %maximum_select_fusion.5), channel_id=1, source_target_pairs={{0,2},{1,3},{2,0},{3,1},{4,6},{5,7},{6,4},{7,5},{8,10},{9,11},{10,... | collective-permute-start | bytes 6291464 | tf_op jit(solution)/shard_map/ppermute | solution.py:14
  582.6 3.8 copy-start.2
  677.2 3.8 collective-permute-start.8
  681.2 27.6 %collective-permute-start.9 = (bf16[512,512]{1,0:T(8,128)(2,1)S(1)}, bf16[512,512]{1,0:T(8,128)(2,1)S(1)}, u32[]{:S(2)}, u32[]{:S(2)}) collective-permute-start(bf16[512,512]{1,0:T(8,128)(2,1)S(1)} %add_convert_fusion), channel_id=1, source_target_pairs={{0,496},{16,0},{32,16},{48,32},{64,48},{80,64},{96,80},{112,96},{1... | collective-permute-start | bytes 1572872 | tf_op jit(solution)/shard_map/ppermute | solution.py:27
  708.8 3.8 collective-permute-start.10
  712.6 14.6 %collective-permute-start.11 = (bf16[512,512]{1,0:T(8,128)(2,1)S(1)}, bf16[512,512]{1,0:T(8,128)(2,1)S(1)}, u32[]{:S(2)}, u32[]{:S(2)}) collective-permute-start(bf16[512,512]{1,0:T(8,128)(2,1)S(1)} %collective-permute-done.10), channel_id=1, source_target_pairs={{0,16},{16,32},{32,48},{48,64},{64,80},{80,96},{96,112},{112,128},... | collective-permute-start | bytes 1572872 | tf_op jit(solution)/shard_map/ppermute | solution.py:27
